TPU v7x, 128 devices: a whole 4x4x4 slice. The times are simulated.
128 devices in a mesh: dp: 4 (over x), seq: 32 (over z, y, core).
Axes of the slice: x: 4, y: 4, z: 4, core: 2. Of those that a mesh axis runs over, the one named last changes fastest.
Arguments:
- inputs: bfloat16 [16384, 6144], P('seq'), may hold values from -6 to 6
- qkv_weight: bfloat16 [6144, 12288], P(None, ('dp', 'seq')), may hold values from -0.078125 to 0.078125
- log_decay: float32 [32, 16384], P('dp', 'seq'), may hold values from -1 to 0, as said below
- out_gain: float32 [32, 128], P('dp'), may hold values from 0.1 to 1.9
Outputs:
- attended: bfloat16 [16384, 4096], P('seq', 'dp')
Inputs may be any that keep to these rules, and one draw needn't show every extreme that they name: `log_decay`: log of a decay factor, negative at every position.
All inputs are finite; a program needn't handle non-finite values.
Results may differ from a plain program's by a relative error of at most 0.0055.
Values may be sent and summed in bfloat16 or wider, within the bound.
No kernel may reach another device: no remote copies, remote signals or barrier semaphores. Data moves between devices by JAX's collectives and lax.ppermute only.
A program may use at most 128 MiB of HBM per device.

v0:
```python
import jax
import jax.numpy as jnp
from jax import lax
from jax.sharding import PartitionSpec as P


def prefix_2(value, axis, join, neutral):
    count, mine = (lax.axis_size(axis), lax.axis_index(axis))
    pieces = jax.tree.map(lambda part: lax.all_gather(part, axis), value)
    subtotal = jax.tree.map(
        lambda part, zero: jnp.full_like(part, 0) + jnp.asarray(zero, part.dtype), value, neutral
    )

    def turn(position, subtotal):
        longer = join(subtotal, jax.tree.map(lambda part: part[position], pieces))
        return jax.tree.map(lambda new, old: jnp.where(position < mine, new, old), longer, subtotal)

    return lax.fori_loop(0, count - 1, turn, subtotal)


def block_terms(queries, keys, values, block_decay):
    cumulated = jnp.cumsum(block_decay, axis=-1)
    tok_count = queries.shape[-2]
    row_index = jnp.arange(tok_count)[:, None]
    col_index = jnp.arange(tok_count)[None, :]
    causal = row_index >= col_index
    spread = cumulated[:, :, None] - cumulated[:, None, :]
    decay_mask = jnp.where(causal, jnp.exp(jnp.where(causal, spread, 0.0)), 0.0)
    scores = jnp.einsum("htd,hsd->hts", queries, keys, preferred_element_type=jnp.float32)
    weights = (scores * decay_mask).astype(jnp.bfloat16)
    intra_term = jnp.einsum("hts,hsd->htd", weights, values, preferred_element_type=jnp.float32)
    tail_decay = jnp.exp(cumulated[:, -1:] - cumulated)
    keys_decayed = keys.astype(jnp.float32) * tail_decay[:, :, None]
    update = jnp.einsum(
        "hsd,hse->hde", keys_decayed, values.astype(jnp.float32), precision=lax.Precision.HIGHEST
    )
    block_total = cumulated[:, -1]
    queries_decayed = queries.astype(jnp.float32) * jnp.exp(cumulated)[:, :, None]
    return (intra_term, update, block_total, queries_decayed)


def finish_heads(intra_term, queries_decayed, carried, gains):
    outer_term = jnp.einsum(
        "htd,hde->hte", queries_decayed, carried, precision=lax.Precision.HIGHEST
    )
    combined = intra_term + outer_term
    root_mean = lax.rsqrt(jnp.mean(combined * combined, axis=-1, keepdims=True) + 1e-05)
    return combined * root_mean * gains[:, None, :]


def chain_combine(earlier_pair, later_pair):
    return (
        earlier_pair[0] + later_pair[0],
        jnp.exp(later_pair[0])[:, None, None] * earlier_pair[1] + later_pair[1],
    )


def shards(inputs, qkv_weight, log_decay, out_gain):
    tok_count = inputs.shape[0]
    local_heads = out_gain.shape[0]
    head_size = out_gain.shape[1]
    projected = jnp.dot(
        inputs,
        lax.all_gather(qkv_weight, "seq", axis=1, tiled=True),
        preferred_element_type=jnp.float32,
    )
    activated = jax.nn.silu(projected).astype(jnp.bfloat16)
    grouped = jnp.transpose(activated.reshape(tok_count, local_heads, 3, head_size), (2, 1, 0, 3))
    intra_term, update, block_total, queries_decayed = block_terms(
        grouped[0], grouped[1], grouped[2], log_decay
    )
    identity = (jnp.zeros_like(block_total), jnp.zeros_like(update))
    prefix = prefix_2((block_total, update), "seq", chain_combine, identity)
    normed = finish_heads(intra_term, queries_decayed, prefix[1], out_gain)
    return (
        jnp.transpose(normed, (1, 0, 2))
        .reshape(tok_count, local_heads * head_size)
        .astype(jnp.bfloat16)
    )


def solution(mesh):
    in_specs = (P("seq", None), P(None, ("dp", "seq")), P("dp", "seq"), P("dp", None))
    out_specs = P("seq", "dp")
    return jax.shard_map(shards, mesh=mesh, in_specs=in_specs, out_specs=out_specs, check_vma=False)
```

profile of v0, /device:TPU:0, one launch (start us, length us, event | category | flops | bytes accessed | tf_op | source)
XLA Modules:
  0.0 301.2 jit_solution(9660974679958368231)
XLA Ops:
  7.3 2.2 reduce-window.6
  10.1 126.8 %all-gather.5.cloned.1.call-done = bf16[6144,3072]{0,1:T(8,128)(2,1)} async-done(((bf16[6144,96]{0,1:T(8,128)(2,1)}), bf16[6144,3072]{0,1:T(8,128)(2,1)}) %all-gather.5.cloned.1.call-update) | async-done | bytes 37748752 | tf_op jit(solution)/shard_map/all_gather | solution.py:64
  136.8 28.2 %multiply_convert_fusion.1 = bf16[512,3072]{1,0:T(8,128)(2,1)} fusion(bf16[512,6144]{1,0:T(8,128)(2,1)} %param.6, bf16[6144,3072]{0,1:T(8,128)(2,1)} %all-gather.5.cloned.1.call-done), kind=kOutput, calls=%fused_computation.4 | convolution fusion | flops 19335217152 | bytes 47185920 | tf_op jit(solution)/shard_map/dot_general | solution.py:62
  165.0 3.2 %copy.26 = bf16[512,3072]{0,1:T(8,128)(2,1)S(1)} copy(bf16[512,3072]{1,0:T(8,128)(2,1)} %multiply_convert_fusion.1) | data formatting | bytes 6291456 | tf_op jit(solution)/shard_map/convert_element_type | solution.py:67
  168.2 2.8 copy.27
  171.1 4.8 %fusion.7 = f32[8,128,128]{2,1,0:T(8,128)} fusion(f32[8,512]{1,0:T(8,128)S(1)} %subtract_exponential_fusion, bf16[3,8,512,128]{3,2,1,0:T(8,128)(2,1)} %bitcast.51), kind=kOutput, calls=%fused_computation.12 | convolution fusion | flops 806354944 | bytes 2637824 | tf_op jit(solution)/shard_map/hsd,hse->hde/dot_general | solution.py:34
  177.3 67.5 %all-reduce = f32[256]{0:T(256)S(1)} all-reduce(f32[256]{0:T(256)S(1)} %dynamic-update-slice), channel_id=2, replica_groups=mesh['dp'=4,'seq'=32] {'seq'}, use_global_device_ids=true, to_apply=%add | all-reduce | flops 256 | bytes 2048
  245.0 5.7 %fusion.1 = f32[8,512,128]{1,2,0:T(8,128)S(1)} fusion(f32[8,512]{1,0:T(8,128)S(1)} %get-tuple-element.129, pred[512,512]{1,0:T(8,128)(4,1)S(1)} %iota_compare_fusion, bf16[3,8,512,128]{3,2,1,0:T(8,128)(2,1)} %bitcast.52), kind=kOutput, calls=%fused_computation.5 | convolution fusion | flops 1084227584 | bytes 5537792 | tf_op jit(solution)/shard_map/hts,hsd->htd/dot_general | solution.py:31
  250.8 37.9 %while.14 = (s32[]{:T(128)}, f32[8,128,128]{2,1,0:T(8,128)S(1)}, s32[]{:T(128)}, f32[32,8]{1,0:T(8,128)S(1)}, f32[32,8,128,128]{3,2,1,0:T(8,128)}, /*index=5*/s32[]{:T(128)}, s32[]{:T(128)}) while((s32[]{:T(128)}, f32[8,128,128]{2,1,0:T(8,128)S(1)}, s32[]{:T(128)}, f32[32,8]{1,0:T(8,128)S(1)}, f32[32,8,128,128]{3,2,1,0:T(8,128)}, ...), condition=%wide.region_3.4_spmd.clone, body=%wide.region_2.3_spmd.clone.sunk | while | flops 524292 | bytes 1573073 | solution.py:18
  250.8 1.2 fusion.24
  252.0 1.2 fusion.24
  253.3 1.2 fusion.24
  254.5 1.2 fusion.24
  255.7 1.2 fusion.24
  256.9 1.2 fusion.24
  258.2 1.2 fusion.24
  259.4 1.2 fusion.24
  260.6 1.2 fusion.24
  261.8 1.2 fusion.24
  263.1 1.2 fusion.24
  264.3 1.2 fusion.24
  265.5 1.2 fusion.24
  266.7 1.2 fusion.24
  268.0 1.2 fusion.24
  269.2 1.2 fusion.24
  270.4 1.2 fusion.24
  271.6 1.2 fusion.24
  272.9 1.2 fusion.24
  274.1 1.2 fusion.24
  282.6 1.2 fusion.24
  288.7 4.0 %multiply_reduce_fusion = (f32[8,512]{1,0:T(8,128)S(1)}, f32[8,512,128]{1,2,0:T(8,128)S(1)}) fusion(f32[8,512,128]{1,2,0:T(8,128)S(1)} %fusion.1, f32[8,128,128]{2,1,0:T(8,128)S(1)} %get-tuple-element.99, f32[8,512]{1,0:T(8,128)S(1)} %get-tuple-element.128, bf16[3,8,512,128]{3,2,1,0:T(8,128)(2,1)} %bitcast.53), kind=kOutput, calls=%fused_computation.11 | convolution fusion | flops 807923712 | bytes 5799936 | tf_op jit(solution)/shard_map/htd,hde->hte/dot_general | solution.py:43
  293.1 1.3 copy.31
  (64 shorter events, 14.9 us)
Async XLA Ops:
  6.5 130.3 %all-gather.5.cloned.1.call-start = ((), (), s32[]{:S(2)}) async-start(), calls=%async_computation | async-start | bytes 38928384 | tf_op jit(solution)/shard_map/all_gather | solution.py:64
  7.3 243.5 %all-gather.7.cloned.1.call-start = ((), (), s32[]{:S(2)}) async-start(), calls=%async_computation.1 | async-start | bytes 17301504 | tf_op jit(solution)/shard_map/all_gather | solution.py:9
  171.1 4.8 %copy-start.1 = (u32[128]{0:T(128)S(1)}, u32[128]{0:T(128)}, u32[]{:S(2)}) copy-start(u32[128]{0:T(128)} %constant.45) | copy-start | bytes 1540
  288.7 4.0 %copy-start = (f32[8,128]{1,0:T(8,128)S(1)}, f32[8,128]{1,0:T(8,128)}, u32[]{:S(2)}) copy-start(f32[8,128]{1,0:T(8,128)} %param.9) | copy-start | bytes 12292
Sparse Core Ops, SparseCore 0:
  9.6 127.2 all-gather.4
  176.0 72.2 all-gather.6
where the time goes:
time: 303 us; the launch traced here: 301 us
  waiting for transfers between devices  128 us (42%)
  blocking collectives  67.5 us (22%)
  matrix products  42.6 us (14%)
  other arithmetic  39.3 us (13%)
  between operations  14.1 us (5%)
  local copies, waits for them, and re-layouts  9.05 us (3%)
    all_gather x1, waiting for transfers between devices, shards(): lax.all_gather(qkv_weight, 'seq', axis=1, tiled=True)  127 us
    unnamed x1, blocking collectives  67.5 us
    select_n x31, other arithmetic, turn(): jnp.where(position < mine, new, old)  36.5 us
    dot_general x1, matrix products, shards(): jnp.dot(inputs, lax.all_gather(qkv_weight, 'seq', axis=1, tiled=True), pr...  28.2 us
  transfers between devices with their start and end apart: 2, of which 1 were waited for; matrix products, arithmetic and copies ran while one was open for 3% of the time, Pallas kernels for 0%

commit v1 on v0

--- a/solution.py
+++ b/solution.py
@@ -61,7 +61,9 @@
     head_size = out_gain.shape[1]
     projected = jnp.dot(
         inputs,
-        lax.all_gather(qkv_weight, "seq", axis=1, tiled=True),
+        jnp.concatenate(
+            lax.all_to_all(jnp.stack([qkv_weight] * lax.axis_size("seq")), "seq", 0, 0), axis=1
+        ),
         preferred_element_type=jnp.float32,
     )
     activated = jax.nn.silu(projected).astype(jnp.bfloat16)

time: 303 us -> 686 us (2.26)
  waiting for transfers between devices: 128 us -> 492 us
  local copies, waits for them, and re-layouts: 9.05 us -> 22.2 us
  starting transfers between devices: 0.04 us -> 8.74 us
    all_to_all x0 -> x1, waiting for transfers between devices: none -> 491 us  [shards(): lax.all_to_all(jnp.stack([qkv_weight] * lax.axis_size('seq')), 'seq', 0, 0)]
    all_gather x1 -> x0, waiting for transfers between devices: 127 us -> none  [shards(): lax.all_gather(qkv_weight, 'seq', axis=1, tiled=True)]
    another operation x1 -> x2, local copies, waits for them, and re-layouts: 0.01 us -> 13.2 us  [the longest x1 13.2 us: shards(): jnp.stack([qkv_weight] * lax.axis_size('seq'))]
    all_to_all x0 -> x1, starting transfers between devices: none -> 8.7 us  [shards(): lax.all_to_all(jnp.stack([qkv_weight] * lax.axis_size('seq')), 'seq', 0, 0)]
  transfers between devices with their start and end apart: 2 -> 2, of which waited for: 1 -> 1; matrix products, arithmetic and copies ran while one was open for 3% -> 1% of each run, Pallas kernels for 0% -> 0%
where the time goes in v1:
time: 686 us; the launch traced here: 684 us
  waiting for transfers between devices  492 us (72%)
  blocking collectives  65.3 us (10%)
  matrix products  42.7 us (6%)
  other arithmetic  38.1 us (6%)
  local copies, waits for them, and re-layouts  22.2 us (3%)
  between operations  14.2 us (2%)
  starting transfers between devices  8.74 us (1%)
    all_to_all x1, waiting for transfers between devices, shards(): lax.all_to_all(jnp.stack([qkv_weight] * lax.axis_size('seq')), 'seq', 0, 0)  491 us
    unnamed x1, blocking collectives  65.3 us
    select_n x31, other arithmetic, turn(): jnp.where(position < mine, new, old)  36.4 us
    dot_general x1, matrix products, shards(): jnp.dot(inputs, jnp.concatenate(lax.all_to_all(jnp.stack([qkv_weight] * l...  28.2 us
  transfers between devices with their start and end apart: 2, of which 1 were waited for; matrix products, arithmetic and copies ran while one was open for 1% of the time, Pallas kernels for 0%

profile of v1, /device:TPU:0, one launch (start us, length us, event | category | flops | bytes accessed | tf_op | source)
XLA Modules:
  0.0 683.6 jit_solution(14940728624341877715)
XLA Ops:
  6.5 13.2 %stack.2 = bf16[32,6144,96]{1,2,0:T(8,128)(2,1)} broadcast(bf16[6144,96]{0,1:T(8,128)(2,1)} %param.7), dimensions={1,2} | broadcast | bytes 38928384 | tf_op jit(solution)/shard_map/stack | solution.py:65
  19.7 8.7 %all-to-all-start = ((bf16[32,6144,96]{1,2,0:T(8,128)(2,1)}), bf16[32,6144,96]{1,2,0:T(8,128)(2,1)}, u32[]{:S(2)}, u32[]{:S(2)}) async-start(bf16[32,6144,96]{1,2,0:T(8,128)(2,1)} %stack.2), calls=%async_computation | async-start | bytes 75497472 | tf_op jit(solution)/shard_map/all_to_all | solution.py:65
  30.2 491.5 %all-to-all-done = bf16[32,6144,96]{1,2,0:T(8,128)(2,1)} async-done(((bf16[32,6144,96]{1,2,0:T(8,128)(2,1)}), bf16[32,6144,96]{1,2,0:T(8,128)(2,1)}, u32[]{:S(2)}, u32[]{:S(2)}) %all-to-all-start) | async-done | bytes 37748768 | tf_op jit(solution)/shard_map/all_to_all | solution.py:65
  521.6 28.2 %multiply_convert_fusion.1 = bf16[512,3072]{1,0:T(8,128)(2,1)} fusion(bf16[512,6144]{1,0:T(8,128)(2,1)} %param.6, bf16[6144,3072]{0,1:T(8,128)(2,1)} %bitcast.1), kind=kOutput, calls=%fused_computation.4 | convolution fusion | flops 19335217152 | bytes 47185920 | tf_op jit(solution)/shard_map/dot_general | solution.py:62
  549.9 3.2 copy.27
  553.0 2.8 copy.28
  555.9 4.8 fusion.7
  562.2 65.3 %all-reduce = f32[256]{0:T(256)S(1)} all-reduce(f32[256]{0:T(256)S(1)} %dynamic-update-slice), channel_id=2, replica_groups=mesh['dp'=4,'seq'=32] {'seq'}, use_global_device_ids=true, to_apply=%add | all-reduce | flops 256 | bytes 2048
  627.7 5.7 fusion.1
  633.4 37.7 %while.14 = (s32[]{:T(128)}, f32[8,128,128]{2,1,0:T(8,128)S(1)}, s32[]{:T(128)}, f32[32,8]{1,0:T(8,128)S(1)}, f32[32,8,128,128]{3,2,1,0:T(8,128)}, /*index=5*/s32[]{:T(128)}, s32[]{:T(128)}) while((s32[]{:T(128)}, f32[8,128,128]{2,1,0:T(8,128)S(1)}, s32[]{:T(128)}, f32[32,8]{1,0:T(8,128)S(1)}, f32[32,8,128,128]{3,2,1,0:T(8,128)}, ...), condition=%wide.region_3.4_spmd.clone, body=%wide.region_2.3_spmd.clone.sunk | while | flops 524292 | bytes 1573065 | solution.py:18
  633.4 1.2 fusion.24
  634.7 1.2 fusion.24
  635.9 1.2 fusion.24
  638.3 1.2 fusion.24
  639.5 1.2 fusion.24
  640.7 1.2 fusion.24
  641.9 1.2 fusion.24
  644.4 1.2 fusion.24
  646.8 1.2 fusion.24
  649.2 1.2 fusion.24
  651.7 1.2 fusion.24
  654.1 1.2 fusion.24
  656.5 1.2 fusion.24
  659.0 1.2 fusion.24
  661.4 1.2 fusion.24
  662.6 1.2 fusion.24
  663.8 1.2 fusion.24
  665.0 1.2 fusion.24
  667.5 1.2 fusion.24
  669.9 1.2 fusion.24
  671.1 4.0 multiply_reduce_fusion
  675.4 1.3 copy.32
  (66 shorter events, 16.4 us)
Async XLA Ops:
  19.7 8.8 %copy-start = (f32[8,512]{1,0:T(8,128)S(1)}, f32[8,512]{1,0:T(8,128)}, u32[]{:S(2)}) copy-start(f32[8,512]{1,0:T(8,128)} %param.8) | copy-start | bytes 49156
  19.7 501.9 %all-to-all-start = ((bf16[32,6144,96]{1,2,0:T(8,128)(2,1)}), bf16[32,6144,96]{1,2,0:T(8,128)(2,1)}, u32[]{:S(2)}, u32[]{:S(2)}) async-start(bf16[32,6144,96]{1,2,0:T(8,128)(2,1)} %stack.2), calls=%async_computation | async-start | bytes 75497472 | tf_op jit(solution)/shard_map/all_to_all | solution.py:65
  28.4 605.0 %all-gather.4.cloned.1.call-start = ((), (), s32[]{:S(2)}) async-start(), calls=%async_computation.1 | async-start | bytes 17301504 | tf_op jit(solution)/shard_map/all_gather | solution.py:9
  555.9 4.8 copy-start.2
  671.1 4.0 copy-start.1
Sparse Core Ops, SparseCore 0:
  560.8 69.9 all-gather.3
